TPU v7x, 32 devices: a whole 2x2x4 slice. The times are simulated.
32 devices in a mesh: group: 2 (over y), sta: 4 (over z), win: 2 (over x), freq: 2 (over core).
Axes of the slice: x: 2, y: 2, z: 4, core: 2. Of those that a mesh axis runs over, the one named last changes fastest.
Arguments:
- records: float32 [1024, 4, 3600], P(('group', 'sta'), 'win', 'freq'), parts along dimension 0, may hold values from -6 to 6
- valid_counts: int32 [8], P(('group', 'sta')), parts along dimension 0, may hold values from 64 to 128, as said below
- pair_blocks: int32 [8, 2], P('group'), parts along dimension 0, may hold values from 0 to 3, as said below
Outputs:
- pair_spectra: bfloat16 [8, 2, 256, 2, 128, 128], P(('group', 'sta'), 'freq', 'win'), parts along dimension 0
There are 2 independent parts, one for each index of `group`. A program takes and returns all parts, laid end to end along the dimension named above; each array names one. Nothing has to cross between parts.
Inputs may be any that keep to these rules, and one draw needn't show every extreme that they name: The stations of block i at positions below valid_counts[i] are live, the others are masked out. `pair_blocks`: slot k belongs to index k // 1 of sta and names two station blocks.
All inputs are finite; a program needn't handle non-finite values.
Results may differ from a plain program's by a relative error of at most 0.001.
Values may be sent and summed in bfloat16 or wider, within the bound.
A program may use at most 64 MiB of HBM per device.

v0:
```python
import math
import jax
import jax.numpy as jnp
from jax import lax
from jax.sharding import PartitionSpec as P

SAMPLES = 3600
BINS = 512
HALF_WIDTH = 10
TWO_PI = 2.0 * math.pi
AMP_FLOOR = 0.1
PRECISE = lax.Precision.HIGHEST


def padded_2(value, sides, width):
    for axis, dim in sides:
        peers, length = (lax.axis_size(axis), value.shape[dim])
        up = [(i, (i + 1) % peers) for i in range(peers - 1)]
        down = [(j, i) for i, j in up]
        last = lax.slice_in_dim(value, length - width, length, axis=dim)
        first = lax.slice_in_dim(value, 0, width, axis=dim)
        before = lax.ppermute(last, axis, up)
        after = lax.ppermute(first, axis, down)
        value = jnp.concatenate([before, value, after], axis=dim)
    return value


def taper_of(sample_index, length_all):
    edge_len = length_all // 20
    position = jnp.minimum(sample_index, length_all - 1 - sample_index)
    ramped = 0.5 * (1.0 - jnp.cos(math.pi * (position.astype(jnp.float32) + 0.5) / edge_len))
    return jnp.where(position < edge_len, ramped, 1.0)


def dft_tables(bin_start, amount, sample_count, length_all):
    bin_index = bin_start + 1 + lax.broadcasted_iota(jnp.int32, (amount, sample_count), 0)
    sample_index = lax.broadcasted_iota(jnp.int32, (amount, sample_count), 1)
    angles = (bin_index * sample_index % length_all).astype(jnp.float32) * (TWO_PI / length_all)
    weight = taper_of(sample_index, length_all) / math.sqrt(length_all)
    return (jnp.cos(angles) * weight, -jnp.sin(angles) * weight)


def cross_pair(left_block, right_block):
    left_real = left_block[:, :, 0]
    left_imag = left_block[:, :, 1]
    stacked = jnp.stack(
        (jnp.stack((left_real, left_imag), 2), jnp.stack((left_imag, -left_real), 2)), 1
    )
    factor = 1.0 / math.sqrt(left_block.shape[1])
    return jnp.einsum("fpwqa,fwqb->fpab", stacked, right_block, precision=PRECISE) * factor


def local(records, valid_counts, pair_blocks):
    block_size = records.shape[0]
    band_bins = BINS // lax.axis_size("freq")
    first_bin = lax.axis_index("freq") * band_bins
    portion = lax.all_gather(records, "freq", axis=2, tiled=True)
    cos_table, sin_table = dft_tables(first_bin, band_bins, portion.shape[2], SAMPLES)
    real_part = jnp.einsum("kn,swn->kws", cos_table, portion, precision=PRECISE)
    imag_part = jnp.einsum("kn,swn->kws", sin_table, portion, precision=PRECISE)
    spectrum = jnp.stack((real_part, imag_part), 2)
    live_mask = (lax.broadcasted_iota(jnp.int32, (block_size,), 0) < valid_counts[0]).astype(
        jnp.float32
    )
    spectrum = spectrum * live_mask
    magnitude = jnp.sqrt(
        spectrum[:, :, 0] * spectrum[:, :, 0] + spectrum[:, :, 1] * spectrum[:, :, 1]
    )
    padded = padded_2(magnitude, (("freq", 0),), HALF_WIDTH)
    row_index = lax.broadcasted_iota(jnp.int32, (band_bins, band_bins + 2 * HALF_WIDTH), 0)
    col_index = lax.broadcasted_iota(jnp.int32, (band_bins, band_bins + 2 * HALF_WIDTH), 1)
    box_matrix = ((col_index - row_index >= 0) & (col_index - row_index <= 2 * HALF_WIDTH)).astype(
        jnp.float32
    )
    summed = jnp.einsum("ij,jws->iws", box_matrix, padded, precision=PRECISE)
    global_bin = first_bin + lax.broadcasted_iota(jnp.int32, (band_bins,), 0)
    counted = (
        jnp.minimum(global_bin + HALF_WIDTH, BINS - 1) - jnp.maximum(global_bin - HALF_WIDTH, 0) + 1
    ).astype(jnp.float32)
    smooth = summed / counted[:, None, None]
    whitened = spectrum / jnp.maximum(smooth, AMP_FLOOR)[:, :, None, :]
    sta_count = lax.axis_size("sta")
    slots = pair_blocks.shape[0] // sta_count
    my_slots = lax.dynamic_slice_in_dim(pair_blocks, lax.axis_index("sta") * slots, slots, 0)
    held_block = lax.all_to_all(whitened, "win", split_axis=0, concat_axis=1, tiled=True)
    blank_pair = jnp.zeros((slots,) + held_block.shape, jnp.float32)
    carried = (blank_pair, blank_pair)
    portion = lax.all_gather(held_block[None], "sta", axis=0, tiled=True)
    amount = portion.shape[0]
    chosen = []
    for column in range(2):
        wanted = my_slots[:, column]
        inside = (wanted >= 0) & (wanted < amount)
        fetched = jnp.take(portion, jnp.clip(wanted, 0, amount - 1), axis=0)
        chosen.append(jnp.where(inside[:, None, None, None, None], fetched, carried[column]))
    left_blocks = chosen[0]
    right_blocks = chosen[1]
    mixed = jax.vmap(cross_pair)(left_blocks, right_blocks).astype(jnp.bfloat16)
    return mixed[:, None]


def solution(mesh):
    in_specs = (P(("group", "sta"), "win", "freq"), P(("group", "sta")), P("group", None))
    out_specs = P(("group", "sta"), "freq", "win", None, None, None)
    return jax.shard_map(local, mesh=mesh, in_specs=in_specs, out_specs=out_specs, check_vma=False)
```

profile of v0, /device:TPU:0, one launch (start us, length us, event | category | flops | bytes accessed | tf_op | source)
XLA Modules:
  0.0 175.7 jit_solution(15182454830260234039)
XLA Ops:
  6.5 0.0 copy-start
  6.5 0.0 all-gather.3.cloned.1.call-start
  6.5 0.7 all-gather.3.cloned.1.call-update
  7.3 0.0 all-gather.5.cloned.1.call-start
  8.0 0.1 subtract_multiply_fusion
  8.1 16.5 %all-gather.3.cloned.1.call-done = f32[128,2,3600]{0,2,1:T(8,128)} async-done(((f32[128,2,1800]{0,2,1:T(8,128)}), f32[128,2,3600]{0,2,1:T(8,128)}) %all-gather.3.cloned.1.call-update) | async-done | bytes 3686416 | tf_op jit(solution)/shard_map/all_gather | solution.py:57
  24.6 0.0 copy-start.1
  24.6 25.0 %fusion.37 = f32[256,2,1,128]{3,0,1,2:T(8,128)S(1)} fusion(f32[128,2,3600]{0,2,1:T(8,128)} %all-gather.3.cloned.1.call-done, f32[3600]{0:T(1024)S(1)} %subtract_multiply_fusion, s32[256]{0:T(256)S(1)} %iota_add_fusion, pred[3600]{0:T(1024)(128)(4,1)S(1)} %fusion.65), kind=kOutput, calls=%fused_computation.35 | convolution fusion | flops 2843136000 | bytes 3967568 | tf_op jit(solution)/shard_map/kn,swn->kws/dot_general | solution.py:60
  49.6 0.0 copy-done.1
  49.6 21.3 %fusion.34 = f32[256,2,1,128]{3,0,1,2:T(8,128)S(1)} fusion(f32[128,2,3600]{0,2,1:T(8,128)S(1)} %copy-done.1, f32[3600]{0:T(1024)S(1)} %subtract_multiply_fusion, s32[256]{0:T(256)S(1)} %iota_add_fusion, pred[3600]{0:T(1024)(128)(4,1)S(1)} %fusion.65), kind=kOutput, calls=%fused_computation.34 | convolution fusion | flops 2842214400 | bytes 3967568 | tf_op jit(solution)/shard_map/kn,swn->kws/dot_general | solution.py:59
  70.9 0.1 fusion.58
  71.1 2.1 %collective-permute-start = (f32[10,2,128]{2,0,1:T(8,128)S(1)}, f32[10,2,128]{2,0,1:T(8,128)S(1)}, u32[]{:S(2)}, u32[]{:S(2)}) collective-permute-start(f32[10,2,128]{2,0,1:T(8,128)S(1)} %get-tuple-element.21), channel_id=1, source_target_pairs={{0,1},{2,3},{4,5},{6,7},{8,9},{10,11},{12,13},{14,15},{16,17},{18,... | collective-permute-start | bytes 30728 | tf_op jit(solution)/shard_map/ppermute | solution.py:22
  73.2 1.3 collective-permute-start.1
  74.5 0.1 fusion.86
  74.6 0.0 collective-permute-done
  74.6 1.7 collective-permute-done.1
  76.3 0.5 fusion.40
  76.8 0.1 broadcast_divide_fusion
  76.8 0.4 copy.6
  77.3 11.3 %all_to_all.15 = f32[256,2,2,128]{3,1,2,0:T(2,128)S(1)} all-to-all(f32[256,2,2,128]{3,1,2,0:T(2,128)S(1)} %copy.6), channel_id=1, replica_groups=mesh['group'=2,'sta'=4,'win'=2,'freq'=2] {'win'}, dimensions={0} | all-to-all | bytes 1048576 | tf_op jit(solution)/shard_map/all_to_all | solution.py:85
  88.5 0.8 copy.7
  89.3 0.0 all-gather.5.cloned.1.call-update
  89.4 0.0 copy-done
  89.4 0.1 constant_dynamic-slice_fusion.2
  89.4 0.5 fusion.82
  93.5 42.0 %all-gather.5.cloned.1.call-done = f32[4,128,4,2,128]{4,1,3,2,0:T(8,128)} async-done(((f32[1,128,4,2,128]{4,1,3,2,0:T(8,128)}), f32[4,128,4,2,128]{4,1,3,2,0:T(8,128)}) %all-gather.5.cloned.1.call-update) | async-done | bytes 2097168 | tf_op jit(solution)/shard_map/all_gather | solution.py:88
  135.6 1.3 constant_dynamic-slice_fusion
  136.8 0.5 fusion.85
  137.3 0.5 fusion.45
  137.8 0.1 fusion.81
  137.9 0.1 maximum_bitcast_fusion.1
  138.0 30.8 %fusion.1 = bf16[1,1,128,2,128,128]{5,4,3,2,1,0:T(8,128)(2,1)} fusion(f32[1,128,4,2,128]{4,1,3,2,0:T(8,128)S(1)} %get-tuple-element.17, pred[]{:T(512)} %bitcast.23, pred[]{:T(512)} %bitcast.21, f32[1,128,1,4,2,128]{5,3,4,1,2,0:T(4,128)S(1)} %maximum_bitcast_fusion.1, f32[1,128,1,4,2,128]{5,3,4,1,2,0:T(4,128)S(1)} %fusion.85), kind=kOutput, calls=%fused_computation.3 | convolution fusion | flops 411566080 | bytes 9961474 | tf_op jit(solution)/shard_map/vmap(fpwqa,fwqb->fpab)/dot_general | solution.py:50
  (6 shorter events, 0.1 us)
Async XLA Ops:
  6.5 82.8 %copy-start = (s32[4,2]{0,1:T(2,128)S(1)}, s32[4,2]{0,1:T(2,128)}, u32[]{:S(2)}) copy-start(s32[4,2]{0,1:T(2,128)} %param.7) | copy-start | bytes 100
  6.5 18.0 %all-gather.3.cloned.1.call-start = ((), (), s32[]{:S(2)}) async-start(), calls=%async_computation.1 | async-start | bytes 5529600 | tf_op jit(solution)/shard_map/all_gather | solution.py:57
  7.3 128.3 %all-gather.5.cloned.1.call-start = ((), (), s32[]{:S(2)}) async-start(), calls=%async_computation.2 | async-start | bytes 2621440 | tf_op jit(solution)/shard_map/all_gather | solution.py:88
  24.6 25.0 %copy-start.1 = (f32[128,2,3600]{0,2,1:T(8,128)S(1)}, f32[128,2,3600]{0,2,1:T(8,128)}, u32[]{:S(2)}) copy-start(f32[128,2,3600]{0,2,1:T(8,128)} %all-gather.3.cloned.1.call-done) | copy-start | bytes 11059204
  71.1 3.5 %collective-permute-start = (f32[10,2,128]{2,0,1:T(8,128)S(1)}, f32[10,2,128]{2,0,1:T(8,128)S(1)}, u32[]{:S(2)}, u32[]{:S(2)}) collective-permute-start(f32[10,2,128]{2,0,1:T(8,128)S(1)} %get-tuple-element.21), channel_id=1, source_target_pairs={{0,1},{2,3},{4,5},{6,7},{8,9},{10,11},{12,13},{14,15},{16,17},{18,... | collective-permute-start | bytes 30728 | tf_op jit(solution)/shard_map/ppermute | solution.py:22
  73.2 3.1 %collective-permute-start.1 = (f32[10,2,128]{2,0,1:T(8,128)S(1)}, f32[10,2,128]{2,0,1:T(8,128)S(1)}, u32[]{:S(2)}, u32[]{:S(2)}) collective-permute-start(f32[10,2,128]{2,0,1:T(8,128)S(1)} %get-tuple-element.22), channel_id=1, source_target_pairs={{1,0},{3,2},{5,4},{7,6},{9,8},{11,10},{13,12},{15,14},{17,16},{19,... | collective-permute-start | bytes 30728 | tf_op jit(solution)/shard_map/ppermute | solution.py:23
Sparse Core Ops, SparseCore 0:
  8.9 15.6 all-gather.2
  89.5 46.0 all-gather.4
where the time goes:
time: 176 us
  matrix products  77.6 us (44%)
  waiting for transfers between devices  60.9 us (35%)
  between operations  17.8 us (10%)
  blocking collectives  11.3 us (6%)
  starting transfers between devices  3.45 us (2%)
  local copies, waits for them, and re-layouts  3.12 us (2%)
    all_gather x1, waiting for transfers between devices, local(): portion = lax.all_gather(held_block[None], 'sta', axis=0, tiled=True)  42 us
    dot_general x1, matrix products, cross_pair(): jnp.einsum('fpwqa,fwqb->fpab', stacked, right_block, precision=PRECISE)  30.8 us
    dot_general x1, matrix products, local(): imag_part = jnp.einsum('kn,swn->kws', sin_table, portion, precision=PRECISE)  25 us
    dot_general x1, matrix products, local(): real_part = jnp.einsum('kn,swn->kws', cos_table, portion, precision=PRECISE)  21.3 us
    all_gather x1, waiting for transfers between devices, local(): portion = lax.all_gather(records, 'freq', axis=2, tiled=True)  16.5 us
    all_to_all x1, blocking collectives, local(): lax.all_to_all(whitened, 'win', split_axis=0, concat_axis=1, tiled=True)  11.3 us
  transfers between devices with their start and end apart: 4, of which 3 were waited for; matrix products, arithmetic and copies ran while one was open for 0% of the time, Pallas kernels for 0%

commit v1 on v0

--- a/solution.py
+++ b/solution.py
@@ -10,6 +10,18 @@
 TWO_PI = 2.0 * math.pi
 AMP_FLOOR = 0.1
 PRECISE = lax.Precision.HIGHEST
+
+
+def gather_around(array, axis, dim):
+    ways, here, step = (lax.axis_size(axis), lax.axis_index(axis), array.shape[dim])
+    shape = [n * ways if d == dim else n for d, n in enumerate(array.shape)]
+    full = lax.dynamic_update_slice_in_dim(
+        jnp.zeros(shape, array.dtype), array, here * step, axis=dim
+    )
+    for far in range(1, ways):
+        array = lax.ppermute(array, axis, [(d, (d + 1) % ways) for d in range(ways)])
+        full = lax.dynamic_update_slice_in_dim(full, array, (here - far) % ways * step, axis=dim)
+    return full
 
 
 def padded_2(value, sides, width):
@@ -85,7 +97,7 @@
     held_block = lax.all_to_all(whitened, "win", split_axis=0, concat_axis=1, tiled=True)
     blank_pair = jnp.zeros((slots,) + held_block.shape, jnp.float32)
     carried = (blank_pair, blank_pair)
-    portion = lax.all_gather(held_block[None], "sta", axis=0, tiled=True)
+    portion = gather_around(held_block[None], "sta", 0)
     amount = portion.shape[0]
     chosen = []
     for column in range(2):

time: 176 us -> 169 us (0.960)
  waiting for transfers between devices: 60.9 us -> 53.8 us
    all_gather x1 -> x0, waiting for transfers between devices: 42 us -> none  [local(): portion = lax.all_gather(held_block[None], 'sta', axis=0, tiled=True)]
    ppermute x0 -> x3, waiting for transfers between devices: none -> 34.9 us  [gather_around(): lax.ppermute(array, axis, [(d, (d + 1) % ways) for d in range(ways)])]
  transfers between devices with their start and end apart: 4 -> 6, of which waited for: 3 -> 5; matrix products, arithmetic and copies ran while one was open for 0% -> 1% of each run, Pallas kernels for 0% -> 0%
where the time goes in v1:
time: 169 us
  matrix products  77.8 us (46%)
  waiting for transfers between devices  53.8 us (32%)
  between operations  18.1 us (11%)
  blocking collectives  11.2 us (7%)
  starting transfers between devices  5.11 us (3%)
  local copies, waits for them, and re-layouts  1.78 us (1%)
    ppermute x3, waiting for transfers between devices, gather_around(): lax.ppermute(array, axis, [(d, (d + 1) % ways) for d in range(ways)])  34.9 us
    dot_general x1, matrix products, cross_pair(): jnp.einsum('fpwqa,fwqb->fpab', stacked, right_block, precision=PRECISE)  31 us
    dot_general x1, matrix products, local(): imag_part = jnp.einsum('kn,swn->kws', sin_table, portion, precision=PRECISE)  25 us
    dot_general x1, matrix products, local(): real_part = jnp.einsum('kn,swn->kws', cos_table, portion, precision=PRECISE)  21.3 us
    all_gather x1, waiting for transfers between devices, local(): portion = lax.all_gather(records, 'freq', axis=2, tiled=True)  16.5 us
    all_to_all x1, blocking collectives, local(): lax.all_to_all(whitened, 'win', split_axis=0, concat_axis=1, tiled=True)  11.2 us
  transfers between devices with their start and end apart: 6, of which 5 were waited for; matrix products, arithmetic and copies ran while one was open for 1% of the time, Pallas kernels for 0%

profile of v1, /device:TPU:0, one launch (start us, length us, event | category | flops | bytes accessed | tf_op | source)
XLA Modules:
  0.0 168.7 jit_solution(11501678260353202749)
XLA Ops:
  6.5 0.0 copy-start
  6.5 0.0 all-gather.2.cloned.1.call-start
  6.5 0.7 all-gather.2.cloned.1.call-update
  8.0 0.1 subtract_multiply_fusion
  8.0 16.5 %all-gather.2.cloned.1.call-done = f32[128,2,3600]{0,2,1:T(8,128)} async-done(((f32[128,2,1800]{0,2,1:T(8,128)}), f32[128,2,3600]{0,2,1:T(8,128)}) %all-gather.2.cloned.1.call-update) | async-done | bytes 3686416 | tf_op jit(solution)/shard_map/all_gather | solution.py:69
  24.6 0.0 copy-start.1
  24.6 25.0 %fusion.37 = f32[256,2,1,128]{3,0,1,2:T(8,128)S(1)} fusion(f32[128,2,3600]{0,2,1:T(8,128)} %all-gather.2.cloned.1.call-done, f32[3600]{0:T(1024)S(1)} %subtract_multiply_fusion, s32[256]{0:T(256)S(1)} %iota_add_fusion, pred[3600]{0:T(1024)(128)(4,1)S(1)} %fusion.63), kind=kOutput, calls=%fused_computation.35 | convolution fusion | flops 2843136000 | bytes 3967568 | tf_op jit(solution)/shard_map/kn,swn->kws/dot_general | solution.py:72
  49.6 0.0 copy-done.1
  49.6 21.3 %fusion.34 = f32[256,2,1,128]{3,0,1,2:T(8,128)S(1)} fusion(f32[128,2,3600]{0,2,1:T(8,128)S(1)} %copy-done.1, f32[3600]{0:T(1024)S(1)} %subtract_multiply_fusion, s32[256]{0:T(256)S(1)} %iota_add_fusion, pred[3600]{0:T(1024)(128)(4,1)S(1)} %fusion.63), kind=kOutput, calls=%fused_computation.34 | convolution fusion | flops 2842214400 | bytes 3967568 | tf_op jit(solution)/shard_map/kn,swn->kws/dot_general | solution.py:71
  71.0 0.1 fusion.56
  71.1 2.1 %collective-permute-start = (f32[10,2,128]{2,0,1:T(8,128)S(1)}, f32[10,2,128]{2,0,1:T(8,128)S(1)}, u32[]{:S(2)}, u32[]{:S(2)}) collective-permute-start(f32[10,2,128]{2,0,1:T(8,128)S(1)} %get-tuple-element.19), channel_id=1, source_target_pairs={{0,1},{2,3},{4,5},{6,7},{8,9},{10,11},{12,13},{14,15},{16,17},{18,... | collective-permute-start | bytes 30728 | tf_op jit(solution)/shard_map/ppermute | solution.py:34
  73.2 1.3 collective-permute-start.1
  74.5 0.1 fusion.85
  74.6 0.0 collective-permute-done
  74.6 1.7 collective-permute-done.1
  76.3 0.5 fusion.40
  76.8 0.1 broadcast_divide_fusion
  76.8 0.4 copy.6
  77.3 11.2 %all_to_all.15 = f32[256,2,2,128]{3,1,2,0:T(2,128)S(1)} all-to-all(f32[256,2,2,128]{3,1,2,0:T(2,128)S(1)} %copy.6), channel_id=1, replica_groups=mesh['group'=2,'sta'=4,'win'=2,'freq'=2] {'win'}, dimensions={0} | all-to-all | bytes 1048576 | tf_op jit(solution)/shard_map/all_to_all | solution.py:97
  88.4 0.2 copy.7
  88.6 1.7 %collective-permute-start.2 = (f32[1,128,4,2,128]{4,2,3,1,0:T(4,128)S(1)}, f32[1,128,4,2,128]{4,2,3,1,0:T(4,128)S(1)}, u32[]{:S(2)}, u32[]{:S(2)}) collective-permute-start(f32[1,128,4,2,128]{4,2,3,1,0:T(4,128)S(1)} %bitcast.66), channel_id=1, source_target_pairs={{0,4},{4,8},{8,12},{12,0},{1,5},{5,9},{9,13},{13,1},{2,6},{6,10},{... | collective-permute-start | bytes 1572872 | tf_op jit(solution)/shard_map/ppermute | solution.py:22
  90.3 13.1 %collective-permute-done.2 = f32[1,128,4,2,128]{4,2,3,1,0:T(4,128)S(1)} collective-permute-done((f32[1,128,4,2,128]{4,2,3,1,0:T(4,128)S(1)}, f32[1,128,4,2,128]{4,2,3,1,0:T(4,128)S(1)}, u32[]{:S(2)}, u32[]{:S(2)}) %collective-permute-start.2) | collective-permute-done | bytes 524320 | tf_op jit(solution)/shard_map/ppermute | solution.py:22
  103.4 0.0 collective-permute-start.3
  103.5 13.8 %collective-permute-done.3 = f32[1,128,4,2,128]{4,2,3,1,0:T(4,128)S(1)} collective-permute-done((f32[1,128,4,2,128]{4,2,3,1,0:T(4,128)S(1)}, f32[1,128,4,2,128]{4,2,3,1,0:T(4,128)S(1)}, u32[]{:S(2)}, u32[]{:S(2)}) %collective-permute-start.3) | collective-permute-done | bytes 524320 | tf_op jit(solution)/shard_map/ppermute | solution.py:22
  117.3 0.0 collective-permute-start.4
  117.3 0.0 copy-done
  117.3 0.1 constant_dynamic-slice_fusion
  117.4 0.5 fusion.81
  121.8 0.3 broadcast_in_dim.47
  122.1 0.1 constant_dynamic-update-slice_fusion.3
  122.2 0.1 constant_dynamic-update-slice_fusion.2
  122.2 0.1 constant_dynamic-update-slice_fusion.1
  122.3 7.9 %collective-permute-done.4 = f32[1,128,4,2,128]{4,2,3,1,0:T(4,128)S(1)} collective-permute-done((f32[1,128,4,2,128]{4,2,3,1,0:T(4,128)S(1)}, f32[1,128,4,2,128]{4,2,3,1,0:T(4,128)S(1)}, u32[]{:S(2)}, u32[]{:S(2)}) %collective-permute-start.4) | collective-permute-done | bytes 524320 | tf_op jit(solution)/shard_map/ppermute | solution.py:22
  130.2 0.1 constant_dynamic-update-slice_fusion
  130.3 0.1 fusion.84
  130.4 0.1 select_select_fusion.2
  130.6 0.1 fusion.80
  130.7 0.1 maximum_bitcast_fusion.1
  130.8 31.0 %fusion.1 = bf16[1,1,128,2,128,128]{5,4,3,2,1,0:T(8,128)(2,1)} fusion(f32[4,128,4,2,128]{4,2,3,1,0:T(4,128)S(1)} %constant_dynamic-update-slice_fusion, s32[]{:T(128)} %bitcast.25, pred[]{:T(512)} %bitcast.24, pred[]{:T(512)} %bitcast.22, f32[1,128,1,4,2,128]{5,3,4,1,2,0:T(4,128)S(1)} %maximum_bitcast_fusion.1, f32[1,128,1,4,2,128]{5,3,4,1,2,0:T(4,128)S(1)} %fusion.84), kind=kOutput, calls=%fused_computation.3 | convolution fusion | flops 411566080 | bytes 9961478 | tf_op jit(solution)/shard_map/vmap(fpwqa,fwqb->fpab)/dot_general | solution.py:62
  (6 shorter events, 0.1 us)
Async XLA Ops:
  6.5 110.8 %copy-start = (s32[4,2]{0,1:T(2,128)S(1)}, s32[4,2]{0,1:T(2,128)}, u32[]{:S(2)}) copy-start(s32[4,2]{0,1:T(2,128)} %param.7) | copy-start | bytes 100
  6.5 18.0 %all-gather.2.cloned.1.call-start = ((), (), s32[]{:S(2)}) async-start(), calls=%async_computation.1 | async-start | bytes 5529600 | tf_op jit(solution)/shard_map/all_gather | solution.py:69
  24.6 25.0 %copy-start.1 = (f32[128,2,3600]{0,2,1:T(8,128)S(1)}, f32[128,2,3600]{0,2,1:T(8,128)}, u32[]{:S(2)}) copy-start(f32[128,2,3600]{0,2,1:T(8,128)} %all-gather.2.cloned.1.call-done) | copy-start | bytes 11059204
  71.1 3.5 %collective-permute-start = (f32[10,2,128]{2,0,1:T(8,128)S(1)}, f32[10,2,128]{2,0,1:T(8,128)S(1)}, u32[]{:S(2)}, u32[]{:S(2)}) collective-permute-start(f32[10,2,128]{2,0,1:T(8,128)S(1)} %get-tuple-element.19), channel_id=1, source_target_pairs={{0,1},{2,3},{4,5},{6,7},{8,9},{10,11},{12,13},{14,15},{16,17},{18,... | collective-permute-start | bytes 30728 | tf_op jit(solution)/shard_map/ppermute | solution.py:34
  73.2 3.1 %collective-permute-start.1 = (f32[10,2,128]{2,0,1:T(8,128)S(1)}, f32[10,2,128]{2,0,1:T(8,128)S(1)}, u32[]{:S(2)}, u32[]{:S(2)}) collective-permute-start(f32[10,2,128]{2,0,1:T(8,128)S(1)} %get-tuple-element.20), channel_id=1, source_target_pairs={{1,0},{3,2},{5,4},{7,6},{9,8},{11,10},{13,12},{15,14},{17,16},{19,... | collective-permute-start | bytes 30728 | tf_op jit(solution)/shard_map/ppermute | solution.py:35
  88.6 14.8 %collective-permute-start.2 = (f32[1,128,4,2,128]{4,2,3,1,0:T(4,128)S(1)}, f32[1,128,4,2,128]{4,2,3,1,0:T(4,128)S(1)}, u32[]{:S(2)}, u32[]{:S(2)}) collective-permute-start(f32[1,128,4,2,128]{4,2,3,1,0:T(4,128)S(1)} %bitcast.66), channel_id=1, source_target_pairs={{0,4},{4,8},{8,12},{12,0},{1,5},{5,9},{9,13},{13,1},{2,6},{6,10},{... | collective-permute-start | bytes 1572872 | tf_op jit(solution)/shard_map/ppermute | solution.py:22
  103.4 13.8 %collective-permute-start.3 = (f32[1,128,4,2,128]{4,2,3,1,0:T(4,128)S(1)}, f32[1,128,4,2,128]{4,2,3,1,0:T(4,128)S(1)}, u32[]{:S(2)}, u32[]{:S(2)}) collective-permute-start(f32[1,128,4,2,128]{4,2,3,1,0:T(4,128)S(1)} %collective-permute-done.2), channel_id=1, source_target_pairs={{0,4},{4,8},{8,12},{12,0},{1,5},{5,9},{9,13},{13,1},{2,6},{6,10},{... | collective-permute-start | bytes 1572872 | tf_op jit(solution)/shard_map/ppermute | solution.py:22
  117.3 12.9 %collective-permute-start.4 = (f32[1,128,4,2,128]{4,2,3,1,0:T(4,128)S(1)}, f32[1,128,4,2,128]{4,2,3,1,0:T(4,128)S(1)}, u32[]{:S(2)}, u32[]{:S(2)}) collective-permute-start(f32[1,128,4,2,128]{4,2,3,1,0:T(4,128)S(1)} %collective-permute-done.3), channel_id=1, source_target_pairs={{0,4},{4,8},{8,12},{12,0},{1,5},{5,9},{9,13},{13,1},{2,6},{6,10},{... | collective-permute-start | bytes 1572872 | tf_op jit(solution)/shard_map/ppermute | solution.py:22
Sparse Core Ops, SparseCore 0:
  8.9 15.6 all-gather.1
